TPU v7x, 256 devices: a whole 4x4x8 slice. The times are simulated.
256 devices in a mesh: leaf: 32 (over x_hi, z, core), head: 8 (over x_lo, y).
Axes of the slice: x: 4 (x_hi: 2, x_lo: 2; x = x_hi * 2 + x_lo), y: 4, z: 8, core: 2. Of those that a mesh axis runs over, the one named last changes fastest.
Arguments:
- latents: bfloat16 [2048, 512], P('leaf'), may hold values from -14 to 14
- queries: bfloat16 [4096, 64, 128], P('leaf', 'head'), may hold values from -14 to 14
- grad_out: bfloat16 [4096, 64, 128], P('leaf', 'head'), may hold values from -6 to 6
- key_up_matrix: bfloat16 [64, 128, 512], P('head'), may hold values from -0.25 to 0.25
- value_up_matrix: bfloat16 [64, 512, 128], P('head'), may hold values from -0.25 to 0.25
- parents: int32 [256], replicated, may hold values from 0 to 254, as said below
- branch_node: int32 [32, 8], P('leaf'), may hold values from 0 to 255
- branch_lengths: int32 [32, 8], P('leaf'), may hold values from 1 to 40, 128 in all within a row
Outputs:
- d_queries: bfloat16 [4096, 64, 128], P('leaf', 'head')
- d_latents: float32 [2048, 512], P('leaf')
Inputs may be any that keep to these rules, and one draw needn't show every extreme that they name: parents[0] = 0 and parents[n] < n for every n >= 1.
All inputs are finite; a program needn't handle non-finite values.
Results may differ from a plain program's by a relative error of at most 0.025.
The roundings to bfloat16 on the way count: a program that leaves them out, or rounds other values in their place, can miss the bound.
Values may be sent and summed in bfloat16 or wider, within the bound.
A program may use at most 64 MiB of HBM per device.

v0:
```python
import jax
import jax.numpy as jnp
from jax import lax
from jax.sharding import PartitionSpec as P

NODE_LEN = 8
softmax_scale = 192.0 ** (-0.5)
masked_score = -1e30


def ancestry(parents):
    node_count = parents.shape[0]
    indices = jnp.arange(node_count, dtype=jnp.int32)
    linked = (parents[:, None] == indices[None, :]) | (indices[:, None] == indices[None, :])
    closure = linked.astype(jnp.float32)
    for squaring in range(node_count.bit_length()):
        closure = jnp.minimum(jnp.dot(closure, closure, precision=lax.Precision.HIGHEST), 1.0)
    return closure


def token_nodes(lengths_row, nodes_row, tok_count):
    bounds = jnp.cumsum(lengths_row)
    places = jnp.arange(tok_count, dtype=jnp.int32)
    branch_of = jnp.sum((places[:, None] >= bounds[None, :]).astype(jnp.int32), axis=1)
    select = branch_of[:, None] == jnp.arange(lengths_row.shape[0], dtype=jnp.int32)[None, :]
    return jnp.sum(jnp.where(select, nodes_row[None, :], 0), axis=1)


def live_keys(node_list, closure):
    node_count = closure.shape[0]
    select = (node_list[:, None] == jnp.arange(node_count, dtype=jnp.int32)[None, :]).astype(
        jnp.float32
    )
    reached = jnp.dot(select, closure, precision=lax.Precision.HIGHEST) > 0.5
    return jnp.repeat(reached, NODE_LEN, axis=1)


def on_device(
    latents, queries, grad_out, key_up_matrix, value_up_matrix, parents, branch_node, branch_lengths
):
    closure = ancestry(parents)
    tok_count = queries.shape[0]
    heads_here = queries.shape[1]
    width = latents.shape[1]
    node_list = token_nodes(branch_lengths[0], branch_node[0], tok_count)
    key_live = live_keys(node_list, closure)
    prefix_rows = key_live.shape[1]
    query_latent = jnp.einsum(
        "thd,hdc->thc", queries, key_up_matrix, preferred_element_type=jnp.float32
    ).astype(jnp.bfloat16)
    grad_latent = jnp.einsum(
        "thv,hcv->thc", grad_out, value_up_matrix, preferred_element_type=jnp.float32
    ).astype(jnp.bfloat16)

    def scores(block_keys):
        usable = key_live[:, None, :]
        scaled = (
            jnp.einsum("thc,kc->thk", query_latent, block_keys, preferred_element_type=jnp.float32)
            * softmax_scale
        )
        return (usable, jnp.where(usable, scaled, masked_score))

    forward_start = (
        jnp.full((tok_count, heads_here), masked_score, jnp.float32),
        jnp.zeros((tok_count, heads_here), jnp.float32),
        jnp.zeros((tok_count, heads_here, width), jnp.float32),
    )
    block_keys = lax.all_gather(latents, "leaf", axis=0, tiled=True)

    def advance(state):
        running_max, running_sum, weighted = state
        usable, logits = scores(block_keys)
        new_max = jnp.maximum(running_max, jnp.max(logits, axis=-1))
        weights = jnp.where(usable, jnp.exp(logits - new_max[..., None]), 0.0)
        weighted = jnp.einsum(
            "thk,kc->thc",
            weights.astype(jnp.bfloat16),
            block_keys,
            preferred_element_type=jnp.float32,
        )
        return (new_max, jnp.sum(weights, axis=-1), weighted)

    running_max, running_sum, weighted = advance(forward_start)
    attended = weighted / running_sum[..., None]
    log_norm = running_max + jnp.log(running_sum)
    delta = jnp.sum(grad_latent.astype(jnp.float32) * attended, axis=-1)
    backward_start = (
        jnp.zeros((tok_count, heads_here, width), jnp.float32),
        jnp.zeros((prefix_rows, width), jnp.float32),
    )
    backward_block_keys = lax.all_gather(latents, "leaf", axis=0, tiled=True)

    def advance(state):
        usable, logits = scores(backward_block_keys)
        probs = jnp.where(usable, jnp.exp(logits - log_norm[..., None]), 0.0)
        grad_weights = jnp.einsum(
            "thc,kc->thk", grad_latent, backward_block_keys, preferred_element_type=jnp.float32
        )
        grad_scores = (probs * (grad_weights - delta[..., None])).astype(jnp.bfloat16)
        query_acc = jnp.einsum(
            "thk,kc->thc", grad_scores, backward_block_keys, preferred_element_type=jnp.float32
        )
        contrib = softmax_scale * jnp.einsum(
            "thk,thc->kc", grad_scores, query_latent, preferred_element_type=jnp.float32
        )
        contrib = contrib + jnp.einsum(
            "thk,thc->kc",
            probs.astype(jnp.bfloat16),
            grad_latent,
            preferred_element_type=jnp.float32,
        )
        return (query_acc, contrib)

    query_acc, latent_grad = advance(backward_start)
    query_grad = (softmax_scale * query_acc).astype(jnp.bfloat16)
    d_queries = jnp.einsum(
        "thc,hdc->thd", query_grad, key_up_matrix, preferred_element_type=jnp.float32
    ).astype(jnp.bfloat16)
    owned_rows = lax.psum_scatter(
        latent_grad.astype(jnp.bfloat16), "leaf", scatter_dimension=0, tiled=True
    )
    d_latents = lax.psum(owned_rows, "head").astype(jnp.float32)
    return (d_queries, d_latents)


def solution(mesh):
    placed = (
        P("leaf", None),
        P("leaf", "head", None),
        P("leaf", "head", None),
        P("head", None, None),
        P("head", None, None),
        P(),
        P("leaf", None),
        P("leaf", None),
    )
    return jax.shard_map(
        on_device,
        mesh=mesh,
        in_specs=placed,
        out_specs=(P("leaf", "head", None), P("leaf", None)),
        check_vma=False,
    )
```

profile of v0, /device:TPU:4, one launch (start us, length us, event | category | flops | bytes accessed | tf_op | source)
XLA Modules:
  0.0 321.0 jit_solution(14642406166411518721)
XLA Ops:
  7.2 0.0 copy-start
  7.2 0.0 copy-start.1
  7.2 0.0 all-gather.2.cloned.1.call-start
  7.2 0.7 all-gather.2.cloned.1.call-update
  7.9 0.0 reduce-scatter.2.cloned.1.call-start
  8.0 0.8 reduce-window.8
  8.8 0.1 convert_reduce_fusion
  8.9 0.7 select_reduce_fusion
  9.6 1.0 convolution_minimum_fusion.8
  10.7 0.4 convolution_minimum_fusion.7
  11.1 0.4 convolution_minimum_fusion.6
  11.4 0.4 convolution_minimum_fusion.5
  11.8 0.4 convolution_minimum_fusion.4
  12.2 0.4 convolution_minimum_fusion.3
  12.6 0.4 convolution_minimum_fusion.2
  13.0 0.4 convolution_minimum_fusion.1
  13.4 0.4 convolution_minimum_fusion
  13.8 0.3 convolution_compare_fusion
  14.0 0.1 copy.34
  14.2 0.1 broadcast_bitcast_fusion
  14.3 0.4 copy.35
  14.7 0.0 copy-done
  14.7 1.5 fusion.23
  16.2 0.0 copy-done.1
  16.2 2.4 fusion.24
  18.6 0.0 copy-start.2
  18.6 72.7 %all-gather.2.cloned.1.call-done = bf16[2048,512]{1,0:T(8,128)(2,1)} async-done(((bf16[64,512]{1,0:T(8,128)(2,1)}), bf16[2048,512]{1,0:T(8,128)(2,1)}) %all-gather.2.cloned.1.call-update) | async-done | bytes 2097168 | tf_op jit(solution)/shard_map/all_gather | solution.py:91
  91.3 4.5 %fusion.3 = (f32[128,8]{0,1:T(8,128)S(1)}, f32[128,8,2048]{2,0,1:T(8,128)S(1)}) fusion(pred[128,2048]{1,0:T(8,128)(4,1)S(1)} %copy.35, bf16[128,8,512]{0,2,1:T(8,128)(2,1)S(1)} %fusion.23, bf16[2048,512]{1,0:T(8,128)(2,1)} %all-gather.2.cloned.1.call-done), kind=kOutput, calls=%fused_computation.7 | convolution fusion | flops 2153774080 | bytes 11800576 | tf_op jit(solution)/shard_map/thc,kc->thk/dot_general | solution.py:58
  95.8 2.7 fusion.1
  98.5 0.0 copy-done.2
  98.5 0.0 copy-start.3
  98.5 3.3 %fusion.4 = f32[2048,512,1]{1,0,2:T(8,128)S(1)} fusion(bf16[128,8,512]{0,2,1:T(8,128)(2,1)S(1)} %copy-done.2, f32[128,8,2048]{2,0,1:T(8,128)S(1)} %get-tuple-element.9, f32[128,8]{0,1:T(8,128)S(1)} %log_add_fusion, pred[128,2048]{1,0:T(8,128)(4,1)S(1)} %copy.35), kind=kOutput, calls=%fused_computation.8 | convolution fusion | flops 2157969408 | bytes 13897728 | tf_op jit(solution)/shard_map/thk,thc->kc/dot_general | solution.py:106
  101.7 0.0 copy-done.3
  101.8 2.8 multiply_reduce_fusion
  104.6 5.5 %multiply_convert_fusion = bf16[128,8,2048]{2,0,1:T(8,128)(2,1)S(1)} fusion(f32[128,8,2048]{2,0,1:T(8,128)S(1)} %get-tuple-element.9, f32[128,8]{0,1:T(8,128)S(1)} %multiply_reduce_fusion, f32[128,8]{0,1:T(8,128)S(1)} %log_add_fusion, pred[128,2048]{1,0:T(8,128)(4,1)S(1)} %copy.35, bf16[128,8,512]{0,2,1:T(8,128)(2,1)S(1)} %copy-done.2, ...), kind=kOutput, calls=%fused_computation | convolution fusion | flops 2162163712 | bytes 15998976 | tf_op jit(solution)/shard_map/thc,kc->thk/dot_general | solution.py:96
  110.1 0.0 copy-start.4
  110.1 1.9 copy-done.4
  112.0 4.0 %fusion.6 = bf16[2048,512]{1,0:T(8,128)(2,1)} fusion(f32[2048,512,1]{1,0,2:T(8,128)S(1)} %fusion.4, bf16[128,8,2048]{2,0,1:T(8,128)(2,1)S(1)} %multiply_convert_fusion, bf16[128,8,512]{0,2,1:T(8,128)(2,1)S(1)} %fusion.23), kind=kOutput, calls=%fused_computation.10 | convolution fusion | flops 2150629376 | bytes 11534336 | tf_op jit(solution)/shard_map/thk,thc->kc/dot_general | solution.py:103
  116.0 0.0 reduce-scatter.2.cloned.1.call-update
  116.0 0.0 all-reduce.2.cloned.1.call-start
  116.1 117.2 %reduce-scatter.2.cloned.1.call-done = bf16[64,512]{1,0:T(8,128)(2,1)} async-done(((bf16[2048,512]{1,0:T(8,128)(2,1)}), bf16[64,512]{1,0:T(8,128)(2,1)}) %reduce-scatter.2.cloned.1.call-update) | async-done | bytes 65552 | tf_op jit(solution)/shard_map/reduce_scatter | solution.py:119
  233.3 0.0 all-reduce.2.cloned.1.call-update
  233.3 5.5 %fusion.31 = bf16[128,8,128]{2,0,1:T(8,128)(2,1)S(1)} fusion(bf16[8,128,512]{2,1,0:T(8,128)(2,1)S(1)} %copy-done, bf16[128,8,2048]{2,0,1:T(8,128)(2,1)} %copy-done.4, bf16[2048,512]{1,0:T(8,128)(2,1)} %all-gather.2.cloned.1.call-done), kind=kOutput, calls=%fused_computation.42 | convolution fusion | flops 2282881024 | bytes 7602176 | tf_op jit(solution)/shard_map/thc,hdc->thd/dot_general | solution.py:116
  238.8 0.9 copy.46
  239.6 73.3 %all-reduce.2.cloned.1.call-done = bf16[64,512]{1,0:T(8,128)(2,1)} async-done(((bf16[64,512]{1,0:T(8,128)(2,1)}), bf16[64,512]{1,0:T(8,128)(2,1)}) %all-reduce.2.cloned.1.call-update) | async-done | bytes 65552 | tf_op jit(solution)/shard_map/psum | solution.py:122
  313.0 1.5 convert_element_type.57
  (2 shorter events, 0.0 us)
Async XLA Ops:
  7.2 7.6 %copy-start = (bf16[8,128,512]{2,1,0:T(8,128)(2,1)S(1)}, bf16[8,128,512]{2,1,0:T(8,128)(2,1)}, u32[]{:S(2)}) copy-start(bf16[8,128,512]{2,1,0:T(8,128)(2,1)} %param.11) | copy-start | bytes 3145732
  7.2 9.0 %copy-start.1 = (bf16[8,512,128]{2,1,0:T(8,128)(2,1)S(1)}, bf16[8,512,128]{2,1,0:T(8,128)(2,1)}, u32[]{:S(2)}) copy-start(bf16[8,512,128]{2,1,0:T(8,128)(2,1)} %param.12) | copy-start | bytes 3145732
  7.2 84.1 %all-gather.2.cloned.1.call-start = ((), (), s32[]{:S(2)}) async-start(), calls=%async_computation.1 | async-start | bytes 2162688 | tf_op jit(solution)/shard_map/all_gather | solution.py:91
  7.9 225.3 %reduce-scatter.2.cloned.1.call-start = ((), (), s32[]{:S(2)}) async-start(), calls=%async_computation.2 | async-start | bytes 2162688 | tf_op jit(solution)/shard_map/reduce_scatter | solution.py:119
  18.6 79.9 %copy-start.2 = (bf16[128,8,512]{0,2,1:T(8,128)(2,1)S(1)}, bf16[128,8,512]{0,2,1:T(8,128)(2,1)}, u32[]{:S(2)}) copy-start(bf16[128,8,512]{0,2,1:T(8,128)(2,1)} %fusion.24) | copy-start | bytes 3145732
  98.5 3.3 %copy-start.3 = (bf16[2048,512]{1,0:T(8,128)(2,1)S(1)}, bf16[2048,512]{1,0:T(8,128)(2,1)}, u32[]{:S(2)}) copy-start(bf16[2048,512]{1,0:T(8,128)(2,1)} %all-gather.2.cloned.1.call-done) | copy-start | bytes 6291460
  110.1 1.9 copy-start.4
  116.0 196.9 %all-reduce.2.cloned.1.call-start = ((), (), s32[]{:S(2)}) async-start(), calls=%async_computation.3 | async-start | bytes 131072 | tf_op jit(solution)/shard_map/psum | solution.py:122
Sparse Core Ops, SparseCore 0:
  10.8 80.4 all-gather.1
  116.2 117.0 reduce-scatter.1
  236.1 76.8 all-reduce.1
where the time goes:
time: 321 us
  waiting for transfers between devices  264 us (82%)
  matrix products  33.7 us (10%)
  between operations  14 us (4%)
  other arithmetic  5.85 us (2%)
  local copies, waits for them, and re-layouts  3.47 us (1%)
    reduce_scatter x1, waiting for transfers between devices, on_device(): lax.psum_scatter(latent_grad.astype(jnp.bfloat16), 'leaf', scatter_dimens...  117 us
    psum x1, waiting for transfers between devices, on_device(): d_latents = lax.psum(owned_rows, 'head').astype(jnp.float32)  73.3 us
    all_gather x1, waiting for transfers between devices, on_device(): backward_block_keys = lax.all_gather(latents, 'leaf', axis=0, tiled=True)  72.7 us
  transfers between devices with their start and end apart: 3, of which 3 were waited for; matrix products, arithmetic and copies ran while one was open for 5% of the time, Pallas kernels for 0%

commit v1 on v0

--- a/solution.py
+++ b/solution.py
@@ -6,6 +6,11 @@
 NODE_LEN = 8
 softmax_scale = 192.0 ** (-0.5)
 masked_score = -1e30
+
+
+def add_all(x, axis):
+    parts = lax.all_gather(x, axis)
+    return jnp.sum(parts, axis=0)
 
 
 def ancestry(parents):
@@ -119,7 +124,7 @@
     owned_rows = lax.psum_scatter(
         latent_grad.astype(jnp.bfloat16), "leaf", scatter_dimension=0, tiled=True
     )
-    d_latents = lax.psum(owned_rows, "head").astype(jnp.float32)
+    d_latents = add_all(owned_rows, "head").astype(jnp.float32)
     return (d_queries, d_latents)
 
 

time: 321 us -> 271 us (0.84)
  waiting for transfers between devices: 264 us -> 184 us
  blocking collectives: 0 us -> 29.1 us
    psum x1 -> x0, waiting for transfers between devices: 73.3 us -> none  [on_device(): d_latents = lax.psum(owned_rows, 'head').astype(jnp.float32)]
    all_gather x0 -> x1, blocking collectives: none -> 29.1 us  [add_all(): parts = lax.all_gather(x, axis)]
    reduce_scatter x1, waiting for transfers between devices: 117 us -> 111 us  [on_device(): lax.psum_scatter(latent_grad.astype(jnp.bfloat16), 'leaf', scatter_dimens...]
  transfers between devices with their start and end apart: 3 -> 2, of which waited for: 3 -> 2; matrix products, arithmetic and copies ran while one was open for 5% -> 6% of each run, Pallas kernels for 0% -> 0%
where the time goes in v1:
time: 271 us; the launch traced here: 270 us
  waiting for transfers between devices  184 us (68%)
  matrix products  33.7 us (12%)
  blocking collectives  29.1 us (11%)
  between operations  14.3 us (5%)
  other arithmetic  5.09 us (2%)
  local copies, waits for them, and re-layouts  3.47 us (1%)
    reduce_scatter x1, waiting for transfers between devices, on_device(): lax.psum_scatter(latent_grad.astype(jnp.bfloat16), 'leaf', scatter_dimens...  111 us
    all_gather x1, waiting for transfers between devices, on_device(): backward_block_keys = lax.all_gather(latents, 'leaf', axis=0, tiled=True)  72.7 us
    all_gather x1, blocking collectives, add_all(): parts = lax.all_gather(x, axis)  29.1 us
    dot_general x1, matrix products, advance(): jnp.einsum('thc,kc->thk', grad_latent, backward_block_keys, preferred_ele...  5.48 us
    dot_general x1, matrix products, on_device(): jnp.einsum('thc,hdc->thd', query_grad, key_up_matrix, preferred_element_t...  5.47 us
  transfers between devices with their start and end apart: 2, of which 2 were waited for; matrix products, arithmetic and copies ran while one was open for 6% of the time, Pallas kernels for 0%

profile of v1, /device:TPU:4, one launch (start us, length us, event | category | flops | bytes accessed | tf_op | source)
XLA Modules:
  0.0 269.9 jit_solution(2311044595271952033)
XLA Ops:
  7.2 0.0 copy-start
  7.2 0.0 copy-start.1
  7.2 0.0 all-gather.3.cloned.1.call-start
  7.2 0.7 all-gather.3.cloned.1.call-update
  7.9 0.0 reduce-scatter.2.cloned.1.call-start
  8.0 0.8 reduce-window.8
  8.8 0.1 convert_reduce_fusion
  8.9 0.7 select_reduce_fusion
  9.6 1.0 convolution_minimum_fusion.8
  10.7 0.4 convolution_minimum_fusion.7
  11.1 0.4 convolution_minimum_fusion.6
  11.4 0.4 convolution_minimum_fusion.5
  11.8 0.4 convolution_minimum_fusion.4
  12.2 0.4 convolution_minimum_fusion.3
  12.6 0.4 convolution_minimum_fusion.2
  13.0 0.4 convolution_minimum_fusion.1
  13.4 0.4 convolution_minimum_fusion
  13.8 0.3 convolution_compare_fusion
  14.0 0.1 copy.34
  14.2 0.1 broadcast_bitcast_fusion
  14.3 0.4 copy.35
  14.7 0.0 copy-done
  14.7 1.5 fusion.23
  16.2 0.0 copy-done.1
  16.2 2.4 fusion.24
  18.6 0.0 copy-start.2
  18.6 72.7 %all-gather.3.cloned.1.call-done = bf16[2048,512]{1,0:T(8,128)(2,1)} async-done(((bf16[64,512]{1,0:T(8,128)(2,1)}), bf16[2048,512]{1,0:T(8,128)(2,1)}) %all-gather.3.cloned.1.call-update) | async-done | bytes 2097168 | tf_op jit(solution)/shard_map/all_gather | solution.py:96
  91.3 4.5 %fusion.3 = (f32[128,8]{0,1:T(8,128)S(1)}, f32[128,8,2048]{2,0,1:T(8,128)S(1)}) fusion(pred[128,2048]{1,0:T(8,128)(4,1)S(1)} %copy.35, bf16[128,8,512]{0,2,1:T(8,128)(2,1)S(1)} %fusion.23, bf16[2048,512]{1,0:T(8,128)(2,1)} %all-gather.3.cloned.1.call-done), kind=kOutput, calls=%fused_computation.7 | convolution fusion | flops 2153774080 | bytes 11800576 | tf_op jit(solution)/shard_map/thc,kc->thk/dot_general | solution.py:63
  95.8 2.7 fusion.1
  98.5 0.0 copy-done.2
  98.5 0.0 copy-start.3
  98.5 3.3 %fusion.4 = f32[2048,512,1]{1,0,2:T(8,128)S(1)} fusion(bf16[128,8,512]{0,2,1:T(8,128)(2,1)S(1)} %copy-done.2, f32[128,8,2048]{2,0,1:T(8,128)S(1)} %get-tuple-element.9, f32[128,8]{0,1:T(8,128)S(1)} %log_add_fusion, pred[128,2048]{1,0:T(8,128)(4,1)S(1)} %copy.35), kind=kOutput, calls=%fused_computation.8 | convolution fusion | flops 2157969408 | bytes 13897728 | tf_op jit(solution)/shard_map/thk,thc->kc/dot_general | solution.py:111
  101.7 0.0 copy-done.3
  101.8 2.8 %multiply_reduce_fusion = f32[128,8]{0,1:T(8,128)S(1)} fusion(bf16[128,8,512]{0,2,1:T(8,128)(2,1)S(1)} %copy-done.2, f32[128,8]{0,1:T(8,128)S(1)} %fusion.1, bf16[2048,512]{1,0:T(8,128)(2,1)S(1)} %copy-done.3, f32[128,8,2048]{2,0,1:T(8,128)S(1)} %get-tuple-element.9, f32[128,8]{0,1:T(8,128)S(1)} %broadcast_maximum_fusion, pred[128,2048]{1,0:T(8,128)(4,1)S(1)} %copy.35), kind=kOutput, calls=%fused_computation.26 | convolution fusion | flops 2160065536 | bytes 11808768 | tf_op jit(solution)/shard_map/thk,kc->thc/dot_general | solution.py:80
  104.6 5.5 %multiply_convert_fusion = bf16[128,8,2048]{2,0,1:T(8,128)(2,1)S(1)} fusion(f32[128,8,2048]{2,0,1:T(8,128)S(1)} %get-tuple-element.9, f32[128,8]{0,1:T(8,128)S(1)} %multiply_reduce_fusion, f32[128,8]{0,1:T(8,128)S(1)} %log_add_fusion, pred[128,2048]{1,0:T(8,128)(4,1)S(1)} %copy.35, bf16[128,8,512]{0,2,1:T(8,128)(2,1)S(1)} %copy-done.2, ...), kind=kOutput, calls=%fused_computation | convolution fusion | flops 2162163712 | bytes 15998976 | tf_op jit(solution)/shard_map/thc,kc->thk/dot_general | solution.py:101
  110.1 0.0 copy-start.4
  110.1 1.9 copy-done.4
  112.0 4.0 %fusion.6 = bf16[2048,512]{1,0:T(8,128)(2,1)} fusion(f32[2048,512,1]{1,0,2:T(8,128)S(1)} %fusion.4, bf16[128,8,2048]{2,0,1:T(8,128)(2,1)S(1)} %multiply_convert_fusion, bf16[128,8,512]{0,2,1:T(8,128)(2,1)S(1)} %fusion.23), kind=kOutput, calls=%fused_computation.10 | convolution fusion | flops 2150629376 | bytes 11534336 | tf_op jit(solution)/shard_map/thk,thc->kc/dot_general | solution.py:108
  116.0 0.0 reduce-scatter.2.cloned.1.call-update
  116.0 5.5 %fusion.31 = bf16[128,8,128]{2,0,1:T(8,128)(2,1)S(1)} fusion(bf16[8,128,512]{2,1,0:T(8,128)(2,1)S(1)} %copy-done, bf16[128,8,2048]{2,0,1:T(8,128)(2,1)} %copy-done.4, bf16[2048,512]{1,0:T(8,128)(2,1)} %all-gather.3.cloned.1.call-done), kind=kOutput, calls=%fused_computation.42 | convolution fusion | flops 2282881024 | bytes 7602176 | tf_op jit(solution)/shard_map/thc,hdc->thd/dot_general | solution.py:121
  121.5 0.9 copy.46
  122.4 110.9 %reduce-scatter.2.cloned.1.call-done = bf16[64,512]{1,0:T(8,128)(2,1)} async-done(((bf16[2048,512]{1,0:T(8,128)(2,1)}), bf16[64,512]{1,0:T(8,128)(2,1)}) %reduce-scatter.2.cloned.1.call-update) | async-done | bytes 65552 | tf_op jit(solution)/shard_map/reduce_scatter | solution.py:124
  233.3 29.1 %all-gather = bf16[512,512]{1,0:T(8,128)(2,1)S(1)} all-gather(bf16[64,512]{1,0:T(8,128)(2,1)} %reduce-scatter.2.cloned.1.call-done), channel_id=2, replica_groups=mesh['leaf'=32,'head'=8] {'head'}, dimensions={0}, use_global_device_ids=true | all-gather | bytes 589824 | tf_op jit(solution)/shard_map/all_gather | solution.py:12
  262.4 0.1 reduce_sum.52
  262.4 0.7 convert_element_type.59
  (2 shorter events, 0.0 us)
Async XLA Ops:
  7.2 7.6 %copy-start = (bf16[8,128,512]{2,1,0:T(8,128)(2,1)S(1)}, bf16[8,128,512]{2,1,0:T(8,128)(2,1)}, u32[]{:S(2)}) copy-start(bf16[8,128,512]{2,1,0:T(8,128)(2,1)} %param.11) | copy-start | bytes 3145732
  7.2 9.0 %copy-start.1 = (bf16[8,512,128]{2,1,0:T(8,128)(2,1)S(1)}, bf16[8,512,128]{2,1,0:T(8,128)(2,1)}, u32[]{:S(2)}) copy-start(bf16[8,512,128]{2,1,0:T(8,128)(2,1)} %param.12) | copy-start | bytes 3145732
  7.2 84.1 %all-gather.3.cloned.1.call-start = ((), (), s32[]{:S(2)}) async-start(), calls=%async_computation.1 | async-start | bytes 2162688 | tf_op jit(solution)/shard_map/all_gather | solution.py:96
  7.9 225.3 %reduce-scatter.2.cloned.1.call-start = ((), (), s32[]{:S(2)}) async-start(), calls=%async_computation.2 | async-start | bytes 2162688 | tf_op jit(solution)/shard_map/reduce_scatter | solution.py:124
  18.6 79.9 %copy-start.2 = (bf16[128,8,512]{0,2,1:T(8,128)(2,1)S(1)}, bf16[128,8,512]{0,2,1:T(8,128)(2,1)}, u32[]{:S(2)}) copy-start(bf16[128,8,512]{0,2,1:T(8,128)(2,1)} %fusion.24) | copy-start | bytes 3145732
  98.5 3.3 %copy-start.3 = (bf16[2048,512]{1,0:T(8,128)(2,1)S(1)}, bf16[2048,512]{1,0:T(8,128)(2,1)}, u32[]{:S(2)}) copy-start(bf16[2048,512]{1,0:T(8,128)(2,1)} %all-gather.3.cloned.1.call-done) | copy-start | bytes 6291460
  110.1 1.9 copy-start.4
Sparse Core Ops, SparseCore 0:
  10.8 80.4 all-gather.2
  116.2 117.0 reduce-scatter.1
